TPU v7x, 32 devices: a whole 2x2x4 slice. The times are simulated.
32 devices in a mesh: replica: 4 (over y, core), table: 8 (over z, x).
Axes of the slice: x: 2, y: 2, z: 4, core: 2. Of those that a mesh axis runs over, the one named last changes fastest.
Arguments:
- cache: float32 [768, 16384], P('table', 'replica'), may hold values from -6 to 6
- accum: float32 [768, 16384], P('table', 'replica'), may hold values from 0.5 to 8
- row_ids: int32 [4, 8, 128], P('replica'), may hold values from 0 to 4095
- lengths: int32 [4, 8], P('replica'), may hold values from 1 to 128, 614 in all within a row
- seq_slot: int32 [4, 8], P('replica'), may hold values from 0 to 7, each once within a row
- block_mask: int32 [4, 8, 2, 2], P('replica'), may hold values 0 or 1
- cotangent: bfloat16 [4, 1024, 768], P('replica', 'table'), may hold values from -6 to 6
- w_uqkv: bfloat16 [768, 3072], P('replica'), may hold values from -0.21875 to 0.21875
- w_out: bfloat16 [768, 768], P('replica'), may hold values from -0.21875 to 0.21875
- w2_accum: float32 [768, 768], P('replica', 'table'), may hold values from 81.92 to 8192
Outputs:
- cache_new: float32 [768, 16384], P('table', 'replica')
- accum_new: float32 [768, 16384], P('table', 'replica')
- w2_step: float32 [768, 768], P('replica', 'table')
Inputs may be any that keep to these rules, and one draw needn't show every extreme that they name: `lengths`: in every replica group some sequence has length 128. `seq_slot`: each row names every slot once.
All inputs are finite; a program needn't handle non-finite values. No bound on the sum of `block_mask` on one device may be relied on, other than what follows from the above.
Results may differ from a plain program's by a relative error of at most 0.012.
Values may be sent and summed in bfloat16 or wider, within the bound.
A program may use at most 64 MiB of HBM per device.

v0:
```python
from functools import partial
import jax
import jax.numpy as jnp
from jax import lax
from jax.sharding import PartitionSpec as P

D = 768
HEADS = 12
HEAD_DIM = 64
SEQ_DEV = 1
SEQ_LEN = 128
CAP = 128
EPS_NORM = 1e-05
EPS_ATTN = 1e-06
STEP_SIZE = 0.5


def normalize(row_data):
    centred = row_data - jnp.mean(row_data, axis=-1, keepdims=True)
    variance = jnp.mean(centred * centred, axis=-1, keepdims=True)
    return centred / jnp.sqrt(variance + EPS_NORM)


def pattern_mask(lengths_at, blocks_at, seq_len):
    block_count = blocks_at.shape[-1]
    block_width = seq_len // block_count
    places = jnp.arange(seq_len, dtype=jnp.int32)
    block_of = places // block_width
    same_block = block_of[:, None] == block_of[None, :]
    chosen = jnp.repeat(jnp.repeat(blocks_at, block_width, axis=1), block_width, axis=2) > 0
    chosen = chosen | same_block[None]
    causal = places[None, :] <= places[:, None]
    inside = places[None, :] < lengths_at[:, None]
    allowed = chosen & causal[None] & inside[:, :, None] & inside[:, None, :]
    return (allowed.astype(jnp.float32), inside)


def attention_branch(hidden_pre, allowed):
    slot_count = allowed.shape[0]
    seq_len = allowed.shape[1]
    projected = jax.nn.silu(hidden_pre).astype(jnp.bfloat16)
    gate_u = projected[:, :D]
    queries = projected[:, D : 2 * D].reshape(slot_count, seq_len, HEADS, HEAD_DIM)
    key_rows = projected[:, 2 * D : 3 * D].reshape(slot_count, seq_len, HEADS, HEAD_DIM)
    value_rows = projected[:, 3 * D :].reshape(slot_count, seq_len, HEADS, HEAD_DIM)
    scores = jnp.einsum(
        "sihd,sjhd->shij", queries, key_rows, preferred_element_type=jnp.float32
    ) * HEAD_DIM ** (-0.5)
    weights = (jax.nn.silu(scores) * allowed[:, None]).astype(jnp.bfloat16)
    attended = jnp.einsum(
        "shij,sjhd->sihd", weights, value_rows, preferred_element_type=jnp.float32
    )
    attended = attended.reshape(slot_count * seq_len, D)
    centred_att = attended - jnp.mean(attended, axis=-1, keepdims=True)
    inverse_dev = 1.0 / jnp.sqrt(
        jnp.mean(centred_att * centred_att, axis=-1, keepdims=True) + EPS_ATTN
    )
    return centred_att * inverse_dev * gate_u.astype(jnp.float32)


def body(cache, accum, row_ids, lengths, seq_slot, block_mask, cotangent, w_uqkv, w_out, w2_accum):
    tables = lax.axis_size("table")
    table_index = lax.axis_index("table")
    columns = cache.shape[0]
    seq_count = seq_slot.shape[1]
    sequence_ids = jnp.arange(seq_count, dtype=jnp.int32)
    matches = (seq_slot[0][:, None] == sequence_ids[None, :]).astype(jnp.int32)
    seq_at = jnp.sum(sequence_ids[:, None] * matches, axis=0)
    lengths_at = jnp.sum(lengths[0][:, None] * matches, axis=0)
    slot_ids = row_ids[0][seq_at].reshape(-1)
    own_first = table_index * SEQ_DEV
    own_lengths = lax.dynamic_slice_in_dim(lengths_at, own_first, SEQ_DEV, 0)
    own_blocks = lax.dynamic_slice_in_dim(block_mask[0][seq_at], own_first, SEQ_DEV, 0)
    allowed, inside = pattern_mask(own_lengths, own_blocks, SEQ_LEN)
    picked = jnp.take(cache, slot_ids, axis=1).astype(jnp.bfloat16).reshape(columns, tables, CAP)
    arrived = lax.all_to_all(picked, "table", split_axis=1, concat_axis=0, tiled=True)
    embedded = arrived.reshape(D, CAP).T
    row_float = embedded.astype(jnp.float32)
    normed = normalize(row_float).astype(jnp.bfloat16)
    full_uqkv = lax.all_gather(w_uqkv, "replica", axis=0, tiled=True)
    hidden_pre = jnp.dot(normed, full_uqkv, preferred_element_type=jnp.float32)
    live_cot = cotangent[0] * inside.reshape(-1)[:, None].astype(jnp.bfloat16)
    d_gated = lax.dot_general(
        live_cot,
        lax.all_gather(w_out, "replica", axis=0, tiled=True),
        (((1,), (1,)), ((), ())),
        preferred_element_type=jnp.float32,
    )
    gated_raw, branch_vjp = jax.vjp(partial(attention_branch, allowed=allowed), hidden_pre)
    gated = gated_raw.astype(jnp.bfloat16)
    d_hidden = branch_vjp(d_gated)[0].astype(jnp.bfloat16)
    d_normed = lax.dot_general(
        d_hidden, full_uqkv, (((1,), (1,)), ((), ())), preferred_element_type=jnp.float32
    )
    _, norm_vjp = jax.vjp(normalize, row_float)
    row_grad = live_cot.astype(jnp.float32) + norm_vjp(d_normed)[0]
    sending = row_grad.T.reshape(tables, columns, CAP)
    returned = lax.all_to_all(sending, "table", split_axis=0, concat_axis=2, tiled=True).reshape(
        columns, tables * CAP
    )
    grad_cols = jnp.zeros_like(cache).at[:, slot_ids].add(returned)
    accum_next = accum + grad_cols * grad_cols
    cache_next = cache - STEP_SIZE * grad_cols / jnp.sqrt(accum_next)
    full_grad = lax.dot_general(
        gated, live_cot, (((0,), (0,)), ((), ())), preferred_element_type=jnp.float32
    )
    by_columns = lax.psum_scatter(full_grad, "table", scatter_dimension=1, tiled=True)
    summed = lax.psum_scatter(by_columns, "replica", scatter_dimension=0, tiled=True)
    w2_step = summed / jnp.sqrt(w2_accum + summed * summed)
    return (cache_next, accum_next, w2_step)


def solution(mesh):
    return jax.shard_map(
        body,
        mesh=mesh,
        in_specs=(
            P("table", "replica"),
            P("table", "replica"),
            P("replica", None, None),
            P("replica", None),
            P("replica", None),
            P("replica", None, None, None),
            P("replica", "table", None),
            P("replica", None),
            P("replica", None),
            P("replica", "table"),
        ),
        out_specs=(P("table", "replica"), P("table", "replica"), P("replica", "table")),
        check_vma=False,
    )
```

profile of v0, /device:TPU:0, one launch (start us, length us, event | category | flops | bytes accessed | tf_op | source)
XLA Modules:
  0.0 180.1 jit_solution(12258738646778073409)
XLA Ops:
  7.9 1.8 %copy.119 = f32[96,4096]{0,1:T(8,128)S(1)} copy(f32[96,4096]{1,0:T(8,128)} %param.10) | data formatting | bytes 3145728 | tf_op args[0]
  10.5 2.9 %gather_fusion.1 = bf16[1024,96]{1,0:T(8,128)(2,1)S(1)} fusion(f32[96,4096]{0,1:T(8,128)S(1)} %copy.119, s32[1024]{0:T(1024)S(1)} %broadcast_clamp_fusion), kind=kCustom, calls=%fused_computation.1 | custom fusion | bytes 397312 | tf_op jit(solution)/shard_map/jit(_take)/gather | solution.py:75
  14.3 7.3 %all-to-all-start = ((bf16[96,8,128]{2,0,1:T(8,128)(2,1)}), bf16[96,8,128]{2,0,1:T(8,128)(2,1)S(1)}, u32[]{:S(2)}, u32[]{:S(2)}) async-start(bf16[96,8,128]{2,0,1:T(8,128)(2,1)} %select_convert_fusion), calls=%async_computation | async-start | bytes 393216 | tf_op jit(solution)/shard_map/all_to_all | solution.py:76
  25.5 4.1 %all-to-all-done = bf16[96,8,128]{2,0,1:T(8,128)(2,1)S(1)} async-done(((bf16[96,8,128]{2,0,1:T(8,128)(2,1)}), bf16[96,8,128]{2,0,1:T(8,128)(2,1)S(1)}, u32[]{:S(2)}, u32[]{:S(2)}) %all-to-all-start) | async-done | bytes 196640 | tf_op jit(solution)/shard_map/all_to_all | solution.py:76
  30.6 19.1 %all-gather.5.cloned.1.call-done = bf16[768,3072]{1,0:T(8,128)(2,1)} async-done(((bf16[192,3072]{1,0:T(8,128)(2,1)}), bf16[768,3072]{1,0:T(8,128)(2,1)}) %all-gather.5.cloned.1.call-update) | async-done | bytes 4718608 | tf_op jit(solution)/shard_map/all_gather | solution.py:80
  49.7 4.4 %multiply_convert_fusion = (bf16[128,3072]{1,0:T(8,128)(2,1)S(1)}, f32[128,3072]{1,0:T(8,128)}) fusion(bf16[768,3072]{1,0:T(8,128)(2,1)} %all-gather.5.cloned.1.call-done, f32[768,128]{0,1:T(8,128)S(1)} %copy.103, f32[128]{0:T(128)S(1)} %get-tuple-element.31, f32[128]{0:T(128)S(1)} %broadcast_multiply_fusion.1), kind=kOutput, calls=%fused_computation.12 | convolution fusion | flops 606240768 | bytes 7472128 | tf_op jit(solution)/shard_map/dot_general | solution.py:81
  54.1 0.9 copy-done.2
  56.2 1.3 multiply_convert_fusion.1
  57.6 1.0 fusion.52
  60.1 8.7 %all-gather.3.cloned.1.call-done = bf16[768,768]{1,0:T(8,128)(2,1)} async-done(((bf16[192,768]{1,0:T(8,128)(2,1)}), bf16[768,768]{1,0:T(8,128)(2,1)}) %all-gather.3.cloned.1.call-update) | async-done | bytes 1179664 | tf_op jit(solution)/shard_map/all_gather | solution.py:85
  68.8 1.9 %multiply_reduce_fusion = (f32[128]{0:T(128)S(1)}, f32[128,768]{1,0:T(8,128)S(1)}) fusion(f32[128,768]{1,0:T(8,128)S(1)} %copy.110, f32[128]{0:T(128)S(1)} %broadcast_multiply_fusion, bf16[128,3072]{1,0:T(8,128)(2,1)} %copy-done.2, bf16[768,768]{1,0:T(8,128)(2,1)} %all-gather.3.cloned.1.call-done, bf16[1,128,768]{2,1,0:T(8,128)(2,1)S(1)} %copy-done.3, ...), kind=kOutput, calls=%fused_computation.56 | convolution fusion | flops 151584640 | bytes 2360576 | tf_op jit(solution)/shard_map/dot_general | solution.py:83
  71.8 3.0 %fusion.28 = f32[768,768]{0,1:T(8,128)} fusion(f32[128,768]{1,0:T(8,128)S(1)} %copy.110, f32[128]{0:T(128)S(1)} %broadcast_multiply_fusion, f32[128]{0:T(128)S(1)} %get-tuple-element.33, bf16[1,128,768]{2,1,0:T(8,128)(2,1)S(1)} %copy-done.3, bf16[128,3072]{1,0:T(8,128)(2,1)} %copy-done.2, bf16[128]{0:T(256)(128)(2,1)S(1)} %fusion.48), kind=kOutput, calls=%fused_computation.59 | convolution fusion | flops 151584768 | bytes 3147008 | tf_op jit(solution)/shard_map/dot_general | solution.py:104
  74.8 1.8 %fusion.50 = (f32[128]{0:T(128)S(1)}, f32[128,768]{1,0:T(8,128)S(1)}, bf16[128,768]{1,0:T(8,128)(2,1)}) fusion(f32[128]{0:T(128)} %get-tuple-element.32, f32[128,768]{1,0:T(8,128)S(1)} %copy.110, f32[128]{0:T(128)S(1)} %broadcast_multiply_fusion, f32[128]{0:T(128)} %copy-done.12, f32[128,768]{1,0:T(8,128)S(1)} %get-tuple-element.41, ...), kind=kLoop, calls=%fused_computation.111 | loop fusion | flops 1081216 | bytes 1574912 | tf_op jit(solution)/shard_map/transpose(jvp())/reduce_sum | solution.py:54
  77.6 1.8 fusion.11
  79.4 1.1 fusion.54
  80.5 1.8 copy.114
  82.2 1.8 %fusion.55 = bf16[12,128,64]{1,2,0:T(8,128)(2,1)} fusion(bf16[12,128,128]{2,1,0:T(8,128)(2,1)S(1)} %fusion.11, bf16[128,12,64]{0,2,1:T(8,128)(2,1)} %bitcast.125), kind=kOutput, calls=%fused_computation.116 | convolution fusion | flops 25165824 | bytes 786432 | tf_op jit(solution)/shard_map/transpose(jvp(sihd,sjhd->shij))/dot_general | solution.py:46
  84.1 1.7 copy.113
  85.8 1.2 fusion.53
  87.2 5.0 %fusion.25 = (f32[128]{0:T(128)S(1)}, f32[128,768]{1,0:T(8,128)S(1)}) fusion(f32[768,128]{0,1:T(8,128)S(1)} %copy.103, f32[128]{0:T(128)S(1)} %copy-done.23, f32[128]{0:T(128)S(1)} %copy-done.14, bf16[768,3072]{1,0:T(8,128)(2,1)} %all-gather.5.cloned.1.call-done, f32[128,3072]{1,0:T(8,128)} %get-tuple-element.35, bf16[128,768]{1,0:T(8,128)(2,1)} %get-tuple-element.26, ...), kind=kOutput, calls=%fused_computation.53 | convolution fusion | flops 611450752 | bytes 7865856 | tf_op jit(solution)/shard_map/dot_general | solution.py:92
  92.6 0.9 copy.115
  93.5 5.5 %all-to-all-start.1 = ((f32[8,96,128]{2,1,0:T(8,128)}), f32[8,96,128]{2,1,0:T(8,128)S(1)}, u32[]{:S(2)}, u32[]{:S(2)}) async-start(f32[8,96,128]{2,1,0:T(8,128)} %bitcast.40), calls=%async_computation.1 | async-start | bytes 786432 | tf_op jit(solution)/shard_map/all_to_all | solution.py:98
  99.1 2.8 %copy.118 = f32[96,4096]{0,1:T(8,128)} copy(f32[96,4096]{1,0:T(8,128)} %param.11) | data formatting | bytes 3145728 | tf_op args[1]
  102.0 13.1 %all-to-all-done.1 = f32[8,96,128]{2,1,0:T(8,128)S(1)} async-done(((f32[8,96,128]{2,1,0:T(8,128)}), f32[8,96,128]{2,1,0:T(8,128)S(1)}, u32[]{:S(2)}, u32[]{:S(2)}) %all-to-all-start.1) | async-done | bytes 393248 | tf_op jit(solution)/shard_map/all_to_all | solution.py:98
  115.6 7.4 %scatter_custom_fusion = f32[96,4096]{0,1:T(8,128)} fusion(s32[1024]{0:T(1024)S(1)} %bitcast.135, f32[1024,96]{1,0:T(8,128)S(1)} %copy.117, f32[]{:T(128)} %constant.61.clone.1), kind=kCustom, calls=%fused_computation.22 | custom fusion | flops 98304 | bytes 1572868 | tf_op jit(solution)/shard_map/scatter-add | solution.py:101
  123.0 26.4 %reduce-scatter.5.cloned.1.call-done = f32[768,96]{0,1:T(8,128)} async-done(((f32[768,768]{0,1:T(8,128)}), f32[768,96]{0,1:T(8,128)}) %reduce-scatter.5.cloned.1.call-update) | async-done | bytes 294928 | tf_op jit(solution)/shard_map/reduce_scatter | solution.py:107
  149.4 1.9 %copy.124 = f32[768,96]{1,0:T(8,128)} copy(f32[768,96]{0,1:T(8,128)} %reduce-scatter.5.cloned.1.call-done) | data formatting | bytes 589824
  151.3 4.6 %multiply_subtract_fusion = (f32[96,4096]{0,1:T(8,128)}, f32[96,4096]{0,1:T(8,128)}) fusion(f32[96,4096]{0,1:T(8,128)S(1)} %copy.119, f32[96,4096]{0,1:T(8,128)} %scatter_custom_fusion, f32[96,4096]{0,1:T(8,128)} %copy.118), kind=kLoop, calls=%fused_computation.5 | loop fusion | flops 1966080 | bytes 7864320 | tf_op jit(solution)/shard_map/sub | solution.py:103
  156.0 2.9 %copy.121 = f32[96,4096]{1,0:T(8,128)} copy(f32[96,4096]{0,1:T(8,128)} %get-tuple-element.20) | data formatting | bytes 3145728
  158.9 1.7 copy.122
  160.6 11.2 %reduce-scatter.7.cloned.1.call-done = f32[192,96]{1,0:T(8,128)} async-done(((f32[768,96]{1,0:T(8,128)}), f32[192,96]{1,0:T(8,128)}) %reduce-scatter.7.cloned.1.call-update) | async-done | bytes 73744
  171.8 1.0 copy.125
  (104 shorter events, 13.9 us)
Async XLA Ops:
  7.2 2.7 %copy-start = (s32[1,8,128]{2,1,0:T(8,128)S(1)}, s32[1,8,128]{2,1,0:T(8,128)}, u32[]{:S(2)}) copy-start(s32[1,8,128]{2,1,0:T(8,128)} %param.12) | copy-start | bytes 12292
  7.2 42.6 %all-gather.5.cloned.1.call-start = ((), (), s32[]{:S(2)}) async-start(), calls=%async_computation.5 | async-start | bytes 5898240 | tf_op jit(solution)/shard_map/all_gather | solution.py:80
  7.9 1.9 %copy-start.21 = (s32[1,8]{1,0:T(1,128)S(1)}, s32[1,8]{1,0:T(1,128)}, u32[]{:S(2)}) copy-start(s32[1,8]{1,0:T(1,128)} %param.13) | copy-start | bytes 100
  7.9 1.9 %copy-start.22 = (s32[1,8]{1,0:T(1,128)S(1)}, s32[1,8]{1,0:T(1,128)}, u32[]{:S(2)}) copy-start(s32[1,8]{1,0:T(1,128)} %param.14) | copy-start | bytes 100
  10.5 11.9 %copy-start.16 = (s32[1,8,2,2]{1,3,2,0:T(2,128)S(1)}, s32[1,8,2,2]{1,3,2,0:T(2,128)}, u32[]{:S(2)}) copy-start(s32[1,8,2,2]{1,3,2,0:T(2,128)} %param.15) | copy-start | bytes 388
  14.3 15.2 %all-to-all-start = ((bf16[96,8,128]{2,0,1:T(8,128)(2,1)}), bf16[96,8,128]{2,0,1:T(8,128)(2,1)S(1)}, u32[]{:S(2)}, u32[]{:S(2)}) async-start(bf16[96,8,128]{2,0,1:T(8,128)(2,1)} %select_convert_fusion), calls=%async_computation | async-start | bytes 393216 | tf_op jit(solution)/shard_map/all_to_all | solution.py:76
  21.6 47.2 %all-gather.3.cloned.1.call-start = ((), (), s32[]{:S(2)}) async-start(), calls=%async_computation.4 | async-start | bytes 1474560 | tf_op jit(solution)/shard_map/all_gather | solution.py:85
  22.3 127.1 %reduce-scatter.5.cloned.1.call-start = ((), (), s32[]{:S(2)}) async-start(), calls=%async_computation.6 | async-start | bytes 2654208 | tf_op jit(solution)/shard_map/reduce_scatter | solution.py:107
  29.9 24.2 %copy-start.13 = (f32[128]{0:T(128)}, f32[128]{0:T(128)S(1)}, u32[]{:S(2)}) copy-start(f32[128]{0:T(128)S(1)} %broadcast_multiply_fusion.1) | copy-start | bytes 1540
  30.1 24.0 %copy-start.19 = (f32[128]{0:T(128)}, f32[128]{0:T(128)S(1)}, u32[]{:S(2)}) copy-start(f32[128]{0:T(128)S(1)} %fusion.23) | copy-start | bytes 1540
  30.6 23.5 %copy-start.17 = (f32[128]{0:T(128)}, f32[128]{0:T(128)S(1)}, u32[]{:S(2)}) copy-start(f32[128]{0:T(128)S(1)} %get-tuple-element.31) | copy-start | bytes 1540
  54.1 0.9 copy-start.2
  56.0 1.5 copy-start.7
  56.2 1.4 copy-start.8
  56.2 1.4 copy-start.6
  57.6 1.0 copy-start.4
  57.6 11.2 %copy-start.3 = (bf16[1,128,768]{2,1,0:T(8,128)(2,1)S(1)}, bf16[1,128,768]{2,1,0:T(8,128)(2,1)}, u32[]{:S(2)}) copy-start(bf16[1,128,768]{2,1,0:T(8,128)(2,1)} %param.16) | copy-start | bytes 589828
  68.8 1.9 %copy-start.15 = (f32[128]{0:T(128)S(1)}, f32[128]{0:T(128)}, u32[]{:S(2)}) copy-start(f32[128]{0:T(128)} %fusion.22) | copy-start | bytes 1540
  71.2 0.6 copy-start.12
  76.9 0.7 copy-start.10
  77.6 1.8 %copy-start.9 = (bf16[128,768]{0,1:T(8,128)(2,1)S(1)}, bf16[128,768]{0,1:T(8,128)(2,1)}, u32[]{:S(2)}) copy-start(bf16[128,768]{0,1:T(8,128)(2,1)} %copy-done.8) | copy-start | bytes 589828
  79.4 6.4 %copy-start.5 = (bf16[12,128,128]{2,1,0:T(8,128)(2,1)S(1)}, bf16[12,128,128]{2,1,0:T(8,128)(2,1)}, u32[]{:S(2)}) copy-start(bf16[12,128,128]{2,1,0:T(8,128)(2,1)} %copy-done.4) | copy-start | bytes 1179652
  80.5 6.7 %copy-start.14 = (f32[128]{0:T(128)S(1)}, f32[128]{0:T(128)}, u32[]{:S(2)}) copy-start(f32[128]{0:T(128)} %copy-done.13) | copy-start | bytes 1540
  80.5 6.7 %copy-start.23 = (f32[128]{0:T(128)S(1)}, f32[128]{0:T(128)}, u32[]{:S(2)}) copy-start(f32[128]{0:T(128)} %get-tuple-element.30) | copy-start | bytes 1540
  87.2 5.0 %copy-start.20 = (f32[128]{0:T(128)S(1)}, f32[128]{0:T(128)}, u32[]{:S(2)}) copy-start(f32[128]{0:T(128)} %copy-done.19) | copy-start | bytes 1540
  87.2 5.0 %copy-start.18 = (f32[128]{0:T(128)S(1)}, f32[128]{0:T(128)}, u32[]{:S(2)}) copy-start(f32[128]{0:T(128)} %copy-done.17) | copy-start | bytes 1540
  93.5 21.6 %all-to-all-start.1 = ((f32[8,96,128]{2,1,0:T(8,128)}), f32[8,96,128]{2,1,0:T(8,128)S(1)}, u32[]{:S(2)}, u32[]{:S(2)}) async-start(f32[8,96,128]{2,1,0:T(8,128)} %bitcast.40), calls=%async_computation.1 | async-start | bytes 786432 | tf_op jit(solution)/shard_map/all_to_all | solution.py:98
  99.0 2.9 %copy-start.11 = (f32[192,96]{1,0:T(8,128)S(1)}, f32[192,96]{1,0:T(8,128)}, u32[]{:S(2)}) copy-start(f32[192,96]{1,0:T(8,128)} %param.19) | copy-start | bytes 221188
  99.0 72.8 %reduce-scatter.7.cloned.1.call-start = ((), (), s32[]{:S(2)}) async-start(), calls=%async_computation.7 | async-start | bytes 491520
  156.0 2.9 %copy-start.1 = (f32[96,4096]{0,1:T(8,128)S(1)}, f32[96,4096]{0,1:T(8,128)}, u32[]{:S(2)}) copy-start(f32[96,4096]{0,1:T(8,128)} %get-tuple-element.21) | copy-start | bytes 4718596
Sparse Core Ops, SparseCore 0:
  9.5 40.1 all-gather.4
  51.3 17.4 all-gather.2
  74.9 74.4 reduce-scatter.4
  151.8 20.0 reduce-scatter.6
where the time goes:
time: 181 us; the launch traced here: 180 us
  waiting for transfers between devices  84 us (46%)
  local copies, waits for them, and re-layouts  27.2 us (15%)
  matrix products  22.4 us (12%)
  other arithmetic  19.4 us (11%)
  between operations  14.2 us (8%)
  starting transfers between devices  12.9 us (7%)
    reduce_scatter x1, waiting for transfers between devices, body(): lax.psum_scatter(full_grad, 'table', scatter_dimension=1, tiled=True)  26.4 us
    all_gather x1, waiting for transfers between devices, body(): full_uqkv = lax.all_gather(w_uqkv, 'replica', axis=0, tiled=True)  19.1 us
    unnamed x57, local copies, waits for them, and re-layouts  15.3 us
    all_to_all x1, waiting for transfers between devices, body(): lax.all_to_all(sending, 'table', split_axis=0, concat_axis=2, tiled=True)  13.1 us
    unnamed x5, waiting for transfers between devices  12.6 us
    all_gather x1, waiting for transfers between devices, body(): lax.all_gather(w_out, 'replica', axis=0, tiled=True)  8.68 us
    scatter-add x1, other arithmetic, body(): grad_cols = jnp.zeros_like(cache).at[:, slot_ids].add(returned)  7.41 us
    all_to_all x1, starting transfers between devices, body(): lax.all_to_all(picked, 'table', split_axis=1, concat_axis=0, tiled=True)  7.28 us
  transfers between devices with their start and end apart: 6, of which 6 were waited for; matrix products, arithmetic and copies ran while one was open for 32% of the time, Pallas kernels for 0%

commit v1 on v0

--- a/solution.py
+++ b/solution.py
@@ -77,7 +77,14 @@
     embedded = arrived.reshape(D, CAP).T
     row_float = embedded.astype(jnp.float32)
     normed = normalize(row_float).astype(jnp.bfloat16)
-    full_uqkv = lax.all_gather(w_uqkv, "replica", axis=0, tiled=True)
+    ring = [w_uqkv]
+    for hop in range(3):
+        ring.append(lax.ppermute(ring[-1], "replica", [(dev, (dev + 1) % 4) for dev in range(4)]))
+    full_uqkv = jnp.roll(
+        jnp.concatenate(ring[::-1], axis=0),
+        (lax.axis_index("replica") + 1) * ring[0].shape[0],
+        axis=0,
+    )
     hidden_pre = jnp.dot(normed, full_uqkv, preferred_element_type=jnp.float32)
     live_cot = cotangent[0] * inside.reshape(-1)[:, None].astype(jnp.bfloat16)
     d_gated = lax.dot_general(

time: 181 us -> 189 us (1.044)
  local copies, waits for them, and re-layouts: 27.2 us -> 38.2 us
  waiting for transfers between devices: 84 us -> 78.6 us
  other arithmetic: 19.4 us -> 23.3 us
    ppermute x0 -> x3, waiting for transfers between devices: none -> 24.9 us  [body(): lax.ppermute(ring[-1], 'replica', [(dev, (dev + 1) % 4) for dev in range(...]
    all_gather x1 -> x0, waiting for transfers between devices: 19.1 us -> none  [body(): full_uqkv = lax.all_gather(w_uqkv, 'replica', axis=0, tiled=True)]
    all_gather x1, waiting for transfers between devices: 8.68 us -> 0.01 us  [body(): lax.all_gather(w_out, 'replica', axis=0, tiled=True)]
    unnamed x57 -> x76, local copies, waits for them, and re-layouts: 15.3 us -> 21.9 us
    all_to_all x1, waiting for transfers between devices: 4.07 us -> 1.43 us  [body(): lax.all_to_all(picked, 'table', split_axis=1, concat_axis=0, tiled=True)]
    unnamed x5 -> x4, waiting for transfers between devices: 12.6 us -> 12.1 us
  transfers between devices with their start and end apart: 6 -> 8, of which waited for: 6 -> 6; matrix products, arithmetic and copies ran while one was open for 32% -> 38% of each run, Pallas kernels for 0% -> 0%
where the time goes in v1:
time: 189 us; the launch traced here: 188 us
  waiting for transfers between devices  78.6 us (42%)
  local copies, waits for them, and re-layouts  38.2 us (20%)
  other arithmetic  23.3 us (12%)
  matrix products  21.6 us (11%)
  between operations  14.3 us (8%)
  starting transfers between devices  12.1 us (6%)
    reduce_scatter x1, waiting for transfers between devices, body(): lax.psum_scatter(full_grad, 'table', scatter_dimension=1, tiled=True)  26.7 us
    ppermute x3, waiting for transfers between devices, body(): lax.ppermute(ring[-1], 'replica', [(dev, (dev + 1) % 4) for dev in range(...  24.9 us
    unnamed x76, local copies, waits for them, and re-layouts  21.9 us
    all_to_all x1, waiting for transfers between devices, body(): lax.all_to_all(sending, 'table', split_axis=0, concat_axis=2, tiled=True)  13.4 us
    unnamed x4, waiting for transfers between devices  12.1 us
    scatter-add x1, other arithmetic, body(): grad_cols = jnp.zeros_like(cache).at[:, slot_ids].add(returned)  7.42 us
    all_to_all x1, starting transfers between devices, body(): lax.all_to_all(picked, 'table', split_axis=1, concat_axis=0, tiled=True)  6.58 us
    dot_general x1, matrix products, body(): lax.dot_general(d_hidden, full_uqkv, (((1,), (1,)), ((), ())), preferred_...  5.33 us
  transfers between devices with their start and end apart: 8, of which 6 were waited for; matrix products, arithmetic and copies ran while one was open for 38% of the time, Pallas kernels for 0%

profile of v1, /device:TPU:0, one launch (start us, length us, event | category | flops | bytes accessed | tf_op | source)
XLA Modules:
  0.0 188.1 jit_solution(15683685219604209176)
XLA Ops:
  7.7 16.0 %collective-permute-done = bf16[192,3072]{1,0:T(8,128)(2,1)S(1)} collective-permute-done((bf16[192,3072]{1,0:T(8,128)(2,1)}, bf16[192,3072]{1,0:T(8,128)(2,1)S(1)}, u32[]{:S(2)}, u32[]{:S(2)}) %collective-permute-start) | collective-permute-done | bytes 1179680 | tf_op jit(solution)/shard_map/ppermute | solution.py:82
  23.8 1.8 copy.119
  26.9 2.9 %gather_fusion.1 = bf16[1024,96]{1,0:T(8,128)(2,1)S(1)} fusion(f32[96,4096]{0,1:T(8,128)S(1)} %copy.119, s32[1024]{0:T(1024)S(1)} %broadcast_clamp_fusion), kind=kCustom, calls=%fused_computation.1 | custom fusion | bytes 397312 | tf_op jit(solution)/shard_map/jit(_take)/gather | solution.py:75
  30.6 8.9 %collective-permute-done.1 = bf16[192,3072]{1,0:T(8,128)(2,1)} collective-permute-done((bf16[192,3072]{1,0:T(8,128)(2,1)S(1)}, bf16[192,3072]{1,0:T(8,128)(2,1)}, u32[]{:S(2)}, u32[]{:S(2)}) %collective-permute-start.1) | collective-permute-done | bytes 1179680 | tf_op jit(solution)/shard_map/ppermute | solution.py:82
  39.5 1.6 select_convert_fusion
  41.2 6.6 %all-to-all-start = ((bf16[96,8,128]{2,0,1:T(8,128)(2,1)}), bf16[96,8,128]{2,0,1:T(8,128)(2,1)S(1)}, u32[]{:S(2)}, u32[]{:S(2)}) async-start(bf16[96,8,128]{2,0,1:T(8,128)(2,1)} %select_convert_fusion), calls=%async_computation | async-start | bytes 393216 | tf_op jit(solution)/shard_map/all_to_all | solution.py:76
  55.0 1.4 all-to-all-done
  57.3 1.9 %copy.103 = f32[768,128]{0,1:T(8,128)} copy(f32[768,128]{1,0:T(8,128)} %bitcast.118) | data formatting | bytes 786432 | tf_op jit(solution)/shard_map/convert_element_type | solution.py:78
  61.0 1.3 constant_dynamic-update-slice_fusion.7
  62.4 1.5 constant_dynamic-update-slice_fusion.6
  64.1 1.4 constant_dynamic-update-slice_fusion.3
  65.4 1.3 constant_dynamic-update-slice_fusion.2
  67.8 3.4 %multiply_convert_fusion = (bf16[128,3072]{1,0:T(8,128)(2,1)S(1)}, f32[128,3072]{1,0:T(8,128)}) fusion(bf16[1536,3072]{1,0:T(8,128)(2,1)S(1)} %constant_dynamic-update-slice_fusion, s32[]{:T(128)S(6)} %select_n.70, f32[768,128]{0,1:T(8,128)S(1)} %copy-done.3, f32[128]{0:T(128)S(1)} %get-tuple-element.31, f32[128]{0:T(128)S(1)} %broadcast_multiply_fusion.1), kind=kOutput, calls=%fused_computation.16 | convolution fusion | flops 606240768 | bytes 7472132 | tf_op jit(solution)/shard_map/dot_general | solution.py:88
  72.7 1.3 multiply_convert_fusion.1
  76.4 2.7 %multiply_reduce_fusion = (f32[128]{0:T(128)S(1)}, f32[128,768]{1,0:T(8,128)}) fusion(f32[128,768]{1,0:T(8,128)S(1)} %copy.110, f32[128]{0:T(128)S(1)} %broadcast_multiply_fusion, bf16[128,3072]{1,0:T(8,128)(2,1)} %copy-done.5, bf16[768,768]{1,0:T(8,128)(2,1)} %all-gather.2.cloned.1.call-done, bf16[1,128,768]{2,1,0:T(8,128)(2,1)S(1)} %copy-done.7, ...), kind=kOutput, calls=%fused_computation.59 | convolution fusion | flops 151584640 | bytes 2360576 | tf_op jit(solution)/shard_map/dot_general | solution.py:90
  80.2 2.0 %fusion.30 = f32[768,768]{0,1:T(8,128)} fusion(f32[128,768]{1,0:T(8,128)S(1)} %copy.110, f32[128]{0:T(128)S(1)} %broadcast_multiply_fusion, f32[128]{0:T(128)S(1)} %get-tuple-element.33, bf16[1,128,768]{2,1,0:T(8,128)(2,1)S(1)} %copy-done.7, bf16[128,3072]{1,0:T(8,128)(2,1)S(1)} %copy-done.6, bf16[128]{0:T(256)(128)(2,1)S(1)} %fusion.52), kind=kOutput, calls=%fused_computation.61 | convolution fusion | flops 151584768 | bytes 3147264 | tf_op jit(solution)/shard_map/dot_general | solution.py:111
  82.2 1.9 %fusion.54 = (f32[128]{0:T(128)S(1)}, f32[128,768]{1,0:T(8,128)S(1)}, bf16[128,768]{1,0:T(8,128)(2,1)}) fusion(f32[128]{0:T(128)} %get-tuple-element.32, f32[128,768]{1,0:T(8,128)S(1)} %copy.110, f32[128]{0:T(128)S(1)} %broadcast_multiply_fusion, f32[128]{0:T(128)} %copy-done.19, f32[128,768]{1,0:T(8,128)} %get-tuple-element.41, ...), kind=kLoop, calls=%fused_computation.123 | loop fusion | flops 1081216 | bytes 1574912 | tf_op jit(solution)/shard_map/transpose(jvp())/reduce_sum | solution.py:54
  85.1 1.8 fusion.14
  88.0 1.7 copy.114
  89.7 1.8 fusion.59
  91.6 1.8 copy.113
  94.7 5.3 %fusion.28 = (f32[128]{0:T(128)S(1)}, f32[128,768]{1,0:T(8,128)S(1)}) fusion(f32[768,128]{0,1:T(8,128)S(1)} %copy-done.4, f32[128]{0:T(128)S(1)} %copy-done.29, f32[128]{0:T(128)S(1)} %copy-done.21, bf16[1536,3072]{1,0:T(8,128)(2,1)} %copy-done.15, s32[]{:T(128)S(6)} %select_n.70, f32[128,3072]{1,0:T(8,128)} %get-tuple-element.35, ...), kind=kOutput, calls=%fused_computation.56 | convolution fusion | flops 611450752 | bytes 7865860 | tf_op jit(solution)/shard_map/dot_general | solution.py:99
  101.4 4.7 %all-to-all-start.1 = ((f32[8,96,128]{2,1,0:T(8,128)}), f32[8,96,128]{2,1,0:T(8,128)S(1)}, u32[]{:S(2)}, u32[]{:S(2)}) async-start(f32[8,96,128]{2,1,0:T(8,128)} %bitcast.40), calls=%async_computation.1 | async-start | bytes 786432 | tf_op jit(solution)/shard_map/all_to_all | solution.py:105
  106.2 2.8 %copy.118 = f32[96,4096]{0,1:T(8,128)} copy(f32[96,4096]{1,0:T(8,128)} %param.11) | data formatting | bytes 3145728 | tf_op args[1]
  109.2 13.4 %all-to-all-done.1 = f32[8,96,128]{2,1,0:T(8,128)S(1)} async-done(((f32[8,96,128]{2,1,0:T(8,128)}), f32[8,96,128]{2,1,0:T(8,128)S(1)}, u32[]{:S(2)}, u32[]{:S(2)}) %all-to-all-start.1) | async-done | bytes 393248 | tf_op jit(solution)/shard_map/all_to_all | solution.py:105
  123.1 7.4 %scatter_custom_fusion = f32[96,4096]{0,1:T(8,128)} fusion(s32[1024]{0:T(1024)S(1)} %bitcast.133, f32[1024,96]{1,0:T(8,128)S(1)} %copy.117, f32[]{:T(128)} %constant.82.clone.1), kind=kCustom, calls=%fused_computation.26 | custom fusion | flops 98304 | bytes 1572868 | tf_op jit(solution)/shard_map/scatter-add | solution.py:108
  130.5 26.7 %reduce-scatter.5.cloned.1.call-done = f32[768,96]{0,1:T(8,128)} async-done(((f32[768,768]{0,1:T(8,128)}), f32[768,96]{0,1:T(8,128)}) %reduce-scatter.5.cloned.1.call-update) | async-done | bytes 294928 | tf_op jit(solution)/shard_map/reduce_scatter | solution.py:114
  157.2 1.9 %copy.124 = f32[768,96]{1,0:T(8,128)} copy(f32[768,96]{0,1:T(8,128)} %reduce-scatter.5.cloned.1.call-done) | data formatting | bytes 589824
  159.1 4.6 %multiply_subtract_fusion = (f32[96,4096]{0,1:T(8,128)}, f32[96,4096]{0,1:T(8,128)}) fusion(f32[96,4096]{0,1:T(8,128)S(1)} %copy.119, f32[96,4096]{0,1:T(8,128)} %scatter_custom_fusion, f32[96,4096]{0,1:T(8,128)} %copy.118), kind=kLoop, calls=%fused_computation.9 | loop fusion | flops 1966080 | bytes 7864320 | tf_op jit(solution)/shard_map/sub | solution.py:110
  163.7 2.9 %copy.121 = f32[96,4096]{1,0:T(8,128)} copy(f32[96,4096]{0,1:T(8,128)} %get-tuple-element.20) | data formatting | bytes 3145728
  166.7 1.7 copy.122
  168.4 11.4 %reduce-scatter.7.cloned.1.call-done = f32[192,96]{1,0:T(8,128)} async-done(((f32[768,96]{1,0:T(8,128)}), f32[192,96]{1,0:T(8,128)}) %reduce-scatter.7.cloned.1.call-update) | async-done | bytes 73744
  (127 shorter events, 25.7 us)
Async XLA Ops:
  7.2 19.1 %copy-start = (s32[1,8,128]{2,1,0:T(8,128)S(1)}, s32[1,8,128]{2,1,0:T(8,128)}, u32[]{:S(2)}) copy-start(s32[1,8,128]{2,1,0:T(8,128)} %param.12) | copy-start | bytes 12292
  7.2 18.5 %copy-start.27 = (s32[1,8]{1,0:T(1,128)S(1)}, s32[1,8]{1,0:T(1,128)}, u32[]{:S(2)}) copy-start(s32[1,8]{1,0:T(1,128)} %param.13) | copy-start | bytes 100
  7.2 18.5 %copy-start.28 = (s32[1,8]{1,0:T(1,128)S(1)}, s32[1,8]{1,0:T(1,128)}, u32[]{:S(2)}) copy-start(s32[1,8]{1,0:T(1,128)} %param.14) | copy-start | bytes 100
  7.2 16.6 %collective-permute-start = (bf16[192,3072]{1,0:T(8,128)(2,1)}, bf16[192,3072]{1,0:T(8,128)(2,1)S(1)}, u32[]{:S(2)}, u32[]{:S(2)}) collective-permute-start(bf16[192,3072]{1,0:T(8,128)(2,1)} %param.17), channel_id=1, source_target_pairs={{0,8},{8,16},{16,24},{24,0},{1,9},{9,17},{17,25},{25,1},{2,10},{10... | collective-permute-start | bytes 3538952 | tf_op jit(solution)/shard_map/ppermute | solution.py:82
  23.8 15.7 %collective-permute-start.1 = (bf16[192,3072]{1,0:T(8,128)(2,1)S(1)}, bf16[192,3072]{1,0:T(8,128)(2,1)}, u32[]{:S(2)}, u32[]{:S(2)}) collective-permute-start(bf16[192,3072]{1,0:T(8,128)(2,1)S(1)} %collective-permute-done), channel_id=1, source_target_pairs={{0,8},{8,16},{16,24},{24,0},{1,9},{9,17},{17,25},{25,1},{2,10},{10... | collective-permute-start | bytes 3538952 | tf_op jit(solution)/shard_map/ppermute | solution.py:82
  39.5 21.5 %collective-permute-start.2 = (bf16[192,3072]{1,0:T(8,128)(2,1)}, bf16[192,3072]{1,0:T(8,128)(2,1)}, u32[]{:S(2)}, u32[]{:S(2)}) collective-permute-start(bf16[192,3072]{1,0:T(8,128)(2,1)} %collective-permute-done.1), channel_id=1, source_target_pairs={{0,8},{8,16},{16,24},{24,0},{1,9},{9,17},{17,25},{25,1},{2,10},{10... | collective-permute-start | bytes 3538952 | tf_op jit(solution)/shard_map/ppermute | solution.py:82
  41.2 15.3 %all-to-all-start = ((bf16[96,8,128]{2,0,1:T(8,128)(2,1)}), bf16[96,8,128]{2,0,1:T(8,128)(2,1)S(1)}, u32[]{:S(2)}, u32[]{:S(2)}) async-start(bf16[96,8,128]{2,0,1:T(8,128)(2,1)} %select_convert_fusion), calls=%async_computation | async-start | bytes 393216 | tf_op jit(solution)/shard_map/all_to_all | solution.py:76
  47.8 28.6 %all-gather.2.cloned.1.call-start = ((), (), s32[]{:S(2)}) async-start(), calls=%async_computation.4 | async-start | bytes 1474560 | tf_op jit(solution)/shard_map/all_gather | solution.py:92
  48.5 108.7 %reduce-scatter.5.cloned.1.call-start = ((), (), s32[]{:S(2)}) async-start(), calls=%async_computation.5 | async-start | bytes 2654208 | tf_op jit(solution)/shard_map/reduce_scatter | solution.py:114
  59.3 7.7 %copy-start.20 = (f32[128]{0:T(128)}, f32[128]{0:T(128)S(1)}, u32[]{:S(2)}) copy-start(f32[128]{0:T(128)S(1)} %broadcast_multiply_fusion.1) | copy-start | bytes 1540
  60.5 3.3 %copy-start.25 = (f32[128]{0:T(128)}, f32[128]{0:T(128)S(1)}, u32[]{:S(2)}) copy-start(f32[128]{0:T(128)S(1)} %fusion.26) | copy-start | bytes 1540
  61.0 6.0 %copy-start.23 = (f32[128]{0:T(128)}, f32[128]{0:T(128)S(1)}, u32[]{:S(2)}) copy-start(f32[128]{0:T(128)S(1)} %get-tuple-element.31) | copy-start | bytes 1540
  62.4 1.6 copy-start.2
  67.0 4.2 %copy-start.15 = (bf16[1536,3072]{1,0:T(8,128)(2,1)}, bf16[1536,3072]{1,0:T(8,128)(2,1)S(1)}, u32[]{:S(2)}) copy-start(bf16[1536,3072]{1,0:T(8,128)(2,1)S(1)} %constant_dynamic-update-slice_fusion) | copy-start | bytes 28311556
  71.2 1.4 copy-start.17
  72.3 1.7 copy-start.10
  72.5 1.5 copy-start.11
  74.0 1.8 copy-start.8
  74.0 2.4 %copy-start.7 = (bf16[1,128,768]{2,1,0:T(8,128)(2,1)S(1)}, bf16[1,128,768]{2,1,0:T(8,128)(2,1)}, u32[]{:S(2)}) copy-start(bf16[1,128,768]{2,1,0:T(8,128)(2,1)} %param.16) | copy-start | bytes 589828
  76.4 3.8 %copy-start.6 = (bf16[128,3072]{1,0:T(8,128)(2,1)S(1)}, bf16[128,3072]{1,0:T(8,128)(2,1)}, u32[]{:S(2)}) copy-start(bf16[128,3072]{1,0:T(8,128)(2,1)} %copy-done.5) | copy-start | bytes 2359300
  76.4 2.7 %copy-start.22 = (f32[128]{0:T(128)S(1)}, f32[128]{0:T(128)}, u32[]{:S(2)}) copy-start(f32[128]{0:T(128)} %fusion.25) | copy-start | bytes 1540
  85.1 1.8 copy-start.13
  86.9 6.4 %copy-start.9 = (bf16[12,128,128]{2,1,0:T(8,128)(2,1)S(1)}, bf16[12,128,128]{2,1,0:T(8,128)(2,1)}, u32[]{:S(2)}) copy-start(bf16[12,128,128]{2,1,0:T(8,128)(2,1)} %copy-done.8) | copy-start | bytes 1179652
  86.9 7.7 %copy-start.4 = (f32[768,128]{0,1:T(8,128)S(1)}, f32[768,128]{0,1:T(8,128)}, u32[]{:S(2)}) copy-start(f32[768,128]{0,1:T(8,128)} %copy.103) | copy-start | bytes 1179652
  86.9 7.7 %copy-start.21 = (f32[128]{0:T(128)S(1)}, f32[128]{0:T(128)}, u32[]{:S(2)}) copy-start(f32[128]{0:T(128)} %copy-done.20) | copy-start | bytes 1540
  86.9 7.7 %copy-start.29 = (f32[128]{0:T(128)S(1)}, f32[128]{0:T(128)}, u32[]{:S(2)}) copy-start(f32[128]{0:T(128)} %get-tuple-element.30) | copy-start | bytes 1540
  94.7 5.4 %copy-start.26 = (f32[128]{0:T(128)S(1)}, f32[128]{0:T(128)}, u32[]{:S(2)}) copy-start(f32[128]{0:T(128)} %copy-done.25) | copy-start | bytes 1540
  94.7 5.4 %copy-start.24 = (f32[128]{0:T(128)S(1)}, f32[128]{0:T(128)}, u32[]{:S(2)}) copy-start(f32[128]{0:T(128)} %copy-done.23) | copy-start | bytes 1540
  101.3 7.7 %copy-start.16 = (f32[192,96]{1,0:T(8,128)S(1)}, f32[192,96]{1,0:T(8,128)}, u32[]{:S(2)}) copy-start(f32[192,96]{1,0:T(8,128)} %param.19) | copy-start | bytes 221188
  101.4 21.2 %all-to-all-start.1 = ((f32[8,96,128]{2,1,0:T(8,128)}), f32[8,96,128]{2,1,0:T(8,128)S(1)}, u32[]{:S(2)}, u32[]{:S(2)}) async-start(f32[8,96,128]{2,1,0:T(8,128)} %bitcast.40), calls=%async_computation.1 | async-start | bytes 786432 | tf_op jit(solution)/shard_map/all_to_all | solution.py:105
  106.0 73.7 %reduce-scatter.7.cloned.1.call-start = ((), (), s32[]{:S(2)}) async-start(), calls=%async_computation.6 | async-start | bytes 491520
  163.7 2.9 %copy-start.1 = (f32[96,4096]{0,1:T(8,128)S(1)}, f32[96,4096]{0,1:T(8,128)}, u32[]{:S(2)}) copy-start(f32[96,4096]{0,1:T(8,128)} %get-tuple-element.21) | copy-start | bytes 4718596
  (6 other events, 5.1 us)
Sparse Core Ops, SparseCore 0:
  50.1 18.8 all-gather.1
  82.3 74.7 reduce-scatter.4
  159.7 20.0 reduce-scatter.6
